TPU v7x, 128 devices: a whole 4x4x4 slice. The times are simulated.
128 devices in a mesh: ctx: 16 (over x, y), tp: 8 (over z, core).
Axes of the slice: x: 4, y: 4, z: 4, core: 2. Of those that a mesh axis runs over, the one named last changes fastest.
Arguments:
- queries: bfloat16 [4096, 8192], P('ctx', 'tp'), may hold values from -160 to 160
- keys: bfloat16 [4096, 1024], P('ctx', 'tp'), may hold values from -4 to 4
- values: bfloat16 [4096, 1024], P('ctx', 'tp'), may hold values from -6 to 6
- positions: int32 [4096], P('ctx'), may hold values from 0 to 4095, as said below
- out_weight: bfloat16 [8192, 8192], P('tp'), may hold values from -0.5 to 0.5
Outputs:
- attn_out: bfloat16 [4096, 8192], P(('ctx', 'tp'))
Inputs may be any that keep to these rules, and one draw needn't show every extreme that they name: positions holds every number of 0 to 4095 once; it is made of 32 runs of 128 rows, each run holding ascending consecutive positions that start at a multiple of 128; the order of the runs is arbitrary.
All inputs are finite; a program needn't handle non-finite values.
Results may differ from a plain program's by a relative error of at most 0.015.
Values may be sent and summed in bfloat16 or wider, within the bound.
No kernel may reach another device: no remote copies, remote signals or barrier semaphores. Data moves between devices by JAX's collectives and lax.ppermute only.
A program may use at most 64 MiB of HBM per device.

v0:
```python
import jax
import jax.numpy as jnp
from jax import lax
from jax.sharding import PartitionSpec as P

HD = 128


def shifted(block, axis, distance):
    devices = range(lax.axis_size(axis))
    route = [((i - distance) % len(devices), i) for i in devices]
    return lax.ppermute(block, axis, route)


def attend(query_block, query_pos, key_block, value_block, key_pos):
    rows_q = query_block.shape[0]
    rows_k = key_block.shape[0]
    groups = key_block.shape[1] // HD
    repeat = query_block.shape[1] // (groups * HD)
    query_heads = query_block.reshape(rows_q, groups, repeat, HD)
    key_heads = key_block.reshape(rows_k, groups, HD)
    value_heads = value_block.reshape(rows_k, groups, HD)
    scores = jnp.einsum(
        "qgrd,kgd->grqk", query_heads, key_heads, preferred_element_type=jnp.float32
    ) * HD ** (-0.5)
    visible = key_pos[None, :] <= query_pos[:, None]
    scores = jnp.where(visible, scores, jnp.float32(-1e30))
    block_max = jnp.max(scores, axis=-1)
    weights = jnp.where(visible, jnp.exp(scores - block_max[..., None]), jnp.float32(0.0))
    block_total = jnp.sum(weights, axis=-1)
    summed = jnp.einsum(
        "grqk,kgd->qgrd",
        weights.astype(jnp.bfloat16),
        value_heads,
        preferred_element_type=jnp.float32,
    )
    scaled = summed / jnp.transpose(jnp.maximum(block_total, 1.0), (2, 0, 1))[..., None]
    block_out = lax.optimization_barrier(
        scaled.reshape(rows_q, groups * repeat * HD).astype(jnp.bfloat16)
    )
    return (
        block_out,
        block_max.reshape(groups * repeat, rows_q),
        block_total.reshape(groups * repeat, rows_q),
    )


def combine_parts(outputs, maxima, totals):
    overall = jnp.max(maxima, axis=0)
    weights = jnp.exp(maxima - overall[None]) * totals
    weights = weights / jnp.sum(weights, axis=0)[None]
    number, tok_rows, head_width = outputs.shape
    head_count = maxima.shape[1]
    spread = outputs.astype(jnp.float32).reshape(
        number, tok_rows, head_count, head_width // head_count
    )
    merged = jnp.sum(spread * jnp.transpose(weights, (0, 2, 1))[..., None], axis=0)
    return merged.reshape(tok_rows, head_width).astype(jnp.bfloat16)


def join_parts(first_part, later):
    return tuple(
        (
            jnp.concatenate([leading[None], trailing], axis=0)
            for leading, trailing in zip(first_part, later)
        )
    )


def attend_block(query_block, query_pos, key_block, value_block, key_pos):
    return attend(query_block, query_pos, key_block, value_block, key_pos)


def on_device(queries, keys, values, positions, out_weight):
    cycle_size = lax.axis_size("ctx")
    device = lax.axis_index("ctx")
    tok_rows = queries.shape[0]
    everywhere = lax.all_gather(positions, "ctx", axis=0, tiled=True)

    def block_positions(owner_index):
        return lax.dynamic_slice_in_dim(everywhere, owner_index * tok_rows, tok_rows, 0)

    first_part = attend_block(queries, positions, keys, values, positions)
    offsets = jnp.arange(1, cycle_size, dtype=jnp.int32)

    def advance_keys(visiting, offset):
        visiting = shifted(visiting, "ctx", 1)
        source = (device - offset) % cycle_size
        return (
            visiting,
            attend_block(queries, positions, visiting[0], visiting[1], block_positions(source)),
        )

    _, later = lax.scan(advance_keys, jnp.stack([keys, values]), offsets)
    outputs, maxima, totals = join_parts(first_part, later)
    merged = combine_parts(outputs, maxima, totals)
    return lax.psum_scatter(
        jnp.dot(merged, out_weight, preferred_element_type=jnp.float32).astype(jnp.bfloat16),
        "tp",
        scatter_dimension=0,
        tiled=True,
    )


def solution(mesh):
    return jax.shard_map(
        on_device,
        mesh=mesh,
        in_specs=(P("ctx", "tp"), P("ctx", "tp"), P("ctx", "tp"), P("ctx"), P("tp", None)),
        out_specs=P(("ctx", "tp"), None),
        check_vma=False,
    )
```

profile of v0, /device:TPU:0, one launch (start us, length us, event | category | flops | bytes accessed | tf_op | source)
XLA Modules:
  0.0 261.6 jit_solution(7151259834409543554)
XLA Ops:
  6.5 0.9 broadcast_compare_fusion.1
  7.4 23.8 %all-gather = s32[16,1,256]{2,1,0:T(1,128)S(1)} all-gather(s32[1,1,256]{2,1,0:T(1,128)} %bitcast.178), channel_id=1, replica_groups=mesh['ctx'=16,'tp'=8] {'ctx'}, dimensions={0}, use_global_device_ids=true | all-gather | bytes 17408 | tf_op jit(solution)/shard_map/all_gather | solution.py:78
  31.2 1.6 fusion.23
  33.4 0.7 fusion.31
  34.4 167.3 %while.18 = (s32[]{:T(128)}, bf16[2,256,128]{2,1,0:T(8,128)(2,1)S(1)}, bf16[15,256,1024]{1,2,0:T(8,128)(2,1)}, f32[15,8,256]{2,1,0:T(8,128)S(1)}, f32[15,8,256]{...) while((s32[]{:T(128)}, ...), condition=%wide.region_5.6_spmd, body=%wide.region_2.5_spmd.sunk | while | flops 275838976 | bytes 9654660 | solution.py:94
  34.4 1.2 collective-permute-start
  37.1 5.7 %collective-permute-done = bf16[2,256,128]{2,1,0:T(8,128)(2,1)S(1)} collective-permute-done((bf16[2,256,128]{2,1,0:T(8,128)(2,1)S(1)}, bf16[2,256,128]{2,1,0:T(8,128)(2,1)S(1)}, u32[]{:S(2)}, u32[]{:S(2)}) %collective-permute-start) | collective-permute-done | bytes 131104 | tf_op jit(solution)/shard_map/while/body/eval_jaxpr/ppermute | solution.py:12
  43.7 0.7 fusion.63
  44.4 0.8 bitcast_dynamic-update-slice_fusion.6
  45.3 0.6 dynamic_slice.15
  46.8 6.8 %collective-permute-done = bf16[2,256,128]{2,1,0:T(8,128)(2,1)S(1)} collective-permute-done((bf16[2,256,128]{2,1,0:T(8,128)(2,1)S(1)}, bf16[2,256,128]{2,1,0:T(8,128)(2,1)S(1)}, u32[]{:S(2)}, u32[]{:S(2)}) %collective-permute-start) | collective-permute-done | bytes 131104 | tf_op jit(solution)/shard_map/while/body/eval_jaxpr/ppermute | solution.py:12
  54.6 0.7 fusion.63
  55.3 0.8 bitcast_dynamic-update-slice_fusion.6
  56.3 0.6 dynamic_slice.15
  57.7 7.2 %collective-permute-done = bf16[2,256,128]{2,1,0:T(8,128)(2,1)S(1)} collective-permute-done((bf16[2,256,128]{2,1,0:T(8,128)(2,1)S(1)}, bf16[2,256,128]{2,1,0:T(8,128)(2,1)S(1)}, u32[]{:S(2)}, u32[]{:S(2)}) %collective-permute-start) | collective-permute-done | bytes 131104 | tf_op jit(solution)/shard_map/while/body/eval_jaxpr/ppermute | solution.py:12
  66.0 0.7 fusion.63
  66.6 0.9 bitcast_dynamic-update-slice_fusion.6
  67.6 0.6 dynamic_slice.15
  69.1 8.0 %collective-permute-done = bf16[2,256,128]{2,1,0:T(8,128)(2,1)S(1)} collective-permute-done((bf16[2,256,128]{2,1,0:T(8,128)(2,1)S(1)}, bf16[2,256,128]{2,1,0:T(8,128)(2,1)S(1)}, u32[]{:S(2)}, u32[]{:S(2)}) %collective-permute-start) | collective-permute-done | bytes 131104 | tf_op jit(solution)/shard_map/while/body/eval_jaxpr/ppermute | solution.py:12
  78.1 0.7 fusion.63
  78.8 0.9 bitcast_dynamic-update-slice_fusion.6
  79.7 0.6 dynamic_slice.15
  81.2 7.2 %collective-permute-done = bf16[2,256,128]{2,1,0:T(8,128)(2,1)S(1)} collective-permute-done((bf16[2,256,128]{2,1,0:T(8,128)(2,1)S(1)}, bf16[2,256,128]{2,1,0:T(8,128)(2,1)S(1)}, u32[]{:S(2)}, u32[]{:S(2)}) %collective-permute-start) | collective-permute-done | bytes 131104 | tf_op jit(solution)/shard_map/while/body/eval_jaxpr/ppermute | solution.py:12
  89.4 0.7 fusion.63
  90.0 0.8 bitcast_dynamic-update-slice_fusion.6
  91.0 0.6 dynamic_slice.15
  92.5 6.8 %collective-permute-done = bf16[2,256,128]{2,1,0:T(8,128)(2,1)S(1)} collective-permute-done((bf16[2,256,128]{2,1,0:T(8,128)(2,1)S(1)}, bf16[2,256,128]{2,1,0:T(8,128)(2,1)S(1)}, u32[]{:S(2)}, u32[]{:S(2)}) %collective-permute-start) | collective-permute-done | bytes 131104 | tf_op jit(solution)/shard_map/while/body/eval_jaxpr/ppermute | solution.py:12
  100.3 0.7 fusion.63
  101.0 0.9 bitcast_dynamic-update-slice_fusion.6
  101.9 0.6 dynamic_slice.15
  103.4 6.8 %collective-permute-done = bf16[2,256,128]{2,1,0:T(8,128)(2,1)S(1)} collective-permute-done((bf16[2,256,128]{2,1,0:T(8,128)(2,1)S(1)}, bf16[2,256,128]{2,1,0:T(8,128)(2,1)S(1)}, u32[]{:S(2)}, u32[]{:S(2)}) %collective-permute-start) | collective-permute-done | bytes 131104 | tf_op jit(solution)/shard_map/while/body/eval_jaxpr/ppermute | solution.py:12
  111.2 0.7 fusion.63
  111.9 0.8 bitcast_dynamic-update-slice_fusion.6
  114.3 6.8 %collective-permute-done = bf16[2,256,128]{2,1,0:T(8,128)(2,1)S(1)} collective-permute-done((bf16[2,256,128]{2,1,0:T(8,128)(2,1)S(1)}, bf16[2,256,128]{2,1,0:T(8,128)(2,1)S(1)}, u32[]{:S(2)}, u32[]{:S(2)}) %collective-permute-start) | collective-permute-done | bytes 131104 | tf_op jit(solution)/shard_map/while/body/eval_jaxpr/ppermute | solution.py:12
  122.1 0.7 fusion.63
  122.8 0.9 bitcast_dynamic-update-slice_fusion.6
  125.2 6.8 %collective-permute-done = bf16[2,256,128]{2,1,0:T(8,128)(2,1)S(1)} collective-permute-done((bf16[2,256,128]{2,1,0:T(8,128)(2,1)S(1)}, bf16[2,256,128]{2,1,0:T(8,128)(2,1)S(1)}, u32[]{:S(2)}, u32[]{:S(2)}) %collective-permute-start) | collective-permute-done | bytes 131104 | tf_op jit(solution)/shard_map/while/body/eval_jaxpr/ppermute | solution.py:12
  133.0 0.7 fusion.63
  133.7 0.8 bitcast_dynamic-update-slice_fusion.6
  134.6 0.6 dynamic_slice.15
  136.1 6.8 %collective-permute-done = bf16[2,256,128]{2,1,0:T(8,128)(2,1)S(1)} collective-permute-done((bf16[2,256,128]{2,1,0:T(8,128)(2,1)S(1)}, bf16[2,256,128]{2,1,0:T(8,128)(2,1)S(1)}, u32[]{:S(2)}, u32[]{:S(2)}) %collective-permute-start) | collective-permute-done | bytes 131104 | tf_op jit(solution)/shard_map/while/body/eval_jaxpr/ppermute | solution.py:12
  143.9 0.7 fusion.63
  144.6 0.9 bitcast_dynamic-update-slice_fusion.6
  145.6 0.6 dynamic_slice.15
  147.0 6.8 %collective-permute-done = bf16[2,256,128]{2,1,0:T(8,128)(2,1)S(1)} collective-permute-done((bf16[2,256,128]{2,1,0:T(8,128)(2,1)S(1)}, bf16[2,256,128]{2,1,0:T(8,128)(2,1)S(1)}, u32[]{:S(2)}, u32[]{:S(2)}) %collective-permute-start) | collective-permute-done | bytes 131104 | tf_op jit(solution)/shard_map/while/body/eval_jaxpr/ppermute | solution.py:12
  154.8 0.7 fusion.63
  155.5 0.8 bitcast_dynamic-update-slice_fusion.6
  157.9 7.3 %collective-permute-done = bf16[2,256,128]{2,1,0:T(8,128)(2,1)S(1)} collective-permute-done((bf16[2,256,128]{2,1,0:T(8,128)(2,1)S(1)}, bf16[2,256,128]{2,1,0:T(8,128)(2,1)S(1)}, u32[]{:S(2)}, u32[]{:S(2)}) %collective-permute-start) | collective-permute-done | bytes 131104 | tf_op jit(solution)/shard_map/while/body/eval_jaxpr/ppermute | solution.py:12
  166.2 0.7 fusion.63
  166.8 0.8 bitcast_dynamic-update-slice_fusion.6
  167.8 0.6 dynamic_slice.15
  169.3 8.1 %collective-permute-done = bf16[2,256,128]{2,1,0:T(8,128)(2,1)S(1)} collective-permute-done((bf16[2,256,128]{2,1,0:T(8,128)(2,1)S(1)}, bf16[2,256,128]{2,1,0:T(8,128)(2,1)S(1)}, u32[]{:S(2)}, u32[]{:S(2)}) %collective-permute-start) | collective-permute-done | bytes 131104 | tf_op jit(solution)/shard_map/while/body/eval_jaxpr/ppermute | solution.py:12
  178.4 0.7 fusion.63
  179.0 0.8 bitcast_dynamic-update-slice_fusion.6
  181.4 6.8 %collective-permute-done = bf16[2,256,128]{2,1,0:T(8,128)(2,1)S(1)} collective-permute-done((bf16[2,256,128]{2,1,0:T(8,128)(2,1)S(1)}, bf16[2,256,128]{2,1,0:T(8,128)(2,1)S(1)}, u32[]{:S(2)}, u32[]{:S(2)}) %collective-permute-start) | collective-permute-done | bytes 131104 | tf_op jit(solution)/shard_map/while/body/eval_jaxpr/ppermute | solution.py:12
  189.3 0.7 fusion.63
  189.9 0.9 bitcast_dynamic-update-slice_fusion.6
  190.9 0.6 dynamic_slice.15
  192.3 6.8 %collective-permute-done = bf16[2,256,128]{2,1,0:T(8,128)(2,1)S(1)} collective-permute-done((bf16[2,256,128]{2,1,0:T(8,128)(2,1)S(1)}, bf16[2,256,128]{2,1,0:T(8,128)(2,1)S(1)}, u32[]{:S(2)}, u32[]{:S(2)}) %collective-permute-start) | collective-permute-done | bytes 131104 | tf_op jit(solution)/shard_map/while/body/eval_jaxpr/ppermute | solution.py:12
  200.2 0.7 fusion.63
  200.8 0.8 bitcast_dynamic-update-slice_fusion.6
  201.8 5.2 %multiply_reduce_fusion = bf16[256,8,128]{0,2,1:T(8,128)(2,1)S(1)} fusion(bf16[15,256,8,128]{1,3,2,0:T(8,128)(2,1)} %bitcast.170, bf16[1,256,8,128]{1,3,2,0:T(8,128)(2,1)S(1)} %bitcast.172, f32[16,256,8]{1,2,0:T(8,128)S(1)} %divide_bitcast_fusion), kind=kLoop, calls=%fused_computation.28 | loop fusion | flops 24903680 | bytes 9043968 | tf_op jit(solution)/shard_map/reduce_sum | solution.py:57
  207.0 12.0 %convolution_convert_fusion = bf16[256,8192]{1,0:T(8,128)(2,1)} fusion(bf16[256,1024]{0,1:T(8,128)(2,1)S(1)} %bitcast.171, bf16[1024,8192]{1,0:T(8,128)(2,1)} %param.11), kind=kOutput, calls=%fused_computation.29 | convolution fusion | flops 4297064448 | bytes 21495808 | tf_op jit(solution)/shard_map/dot_general | solution.py:98
  219.1 35.7 %reduce-scatter.2.cloned.1.call-done = bf16[32,8192]{1,0:T(8,128)(2,1)} async-done(((bf16[256,8192]{1,0:T(8,128)(2,1)}), bf16[32,8192]{1,0:T(8,128)(2,1)}) %reduce-scatter.2.cloned.1.call-update) | async-done | bytes 524304 | tf_op jit(solution)/shard_map/reduce_scatter | solution.py:97
  (130 shorter events, 22.9 us)
Async XLA Ops:
  6.5 248.2 %reduce-scatter.2.cloned.1.call-start = ((), (), s32[]{:S(2)}) async-start(), calls=%async_computation.1 | async-start | bytes 4718592 | tf_op jit(solution)/shard_map/reduce_scatter | solution.py:97
  31.2 2.1 copy-start.3
  33.3 0.8 copy-start.1
  33.4 1.1 copy-start
  33.4 1.1 copy-start.2
  34.4 8.3 %collective-permute-start = (bf16[2,256,128]{2,1,0:T(8,128)(2,1)S(1)}, bf16[2,256,128]{2,1,0:T(8,128)(2,1)S(1)}, u32[]{:S(2)}, u32[]{:S(2)}) collective-permute-start(bf16[2,256,128]{2,1,0:T(8,128)(2,1)S(1)} %get-tuple-element.251), channel_id=1, source_target_pairs={{120,0},{0,8},{8,16},{16,24},{24,32},{32,40},{40,48},{48,56},{56,6... | collective-permute-start | bytes 393224 | tf_op jit(solution)/shard_map/while/body/eval_jaxpr/ppermute | solution.py:12
  45.3 8.4 %collective-permute-start = (bf16[2,256,128]{2,1,0:T(8,128)(2,1)S(1)}, bf16[2,256,128]{2,1,0:T(8,128)(2,1)S(1)}, u32[]{:S(2)}, u32[]{:S(2)}) collective-permute-start(bf16[2,256,128]{2,1,0:T(8,128)(2,1)S(1)} %get-tuple-element.251), channel_id=1, source_target_pairs={{120,0},{0,8},{8,16},{16,24},{24,32},{32,40},{40,48},{48,56},{56,6... | collective-permute-start | bytes 393224 | tf_op jit(solution)/shard_map/while/body/eval_jaxpr/ppermute | solution.py:12
  56.2 8.8 %collective-permute-start = (bf16[2,256,128]{2,1,0:T(8,128)(2,1)S(1)}, bf16[2,256,128]{2,1,0:T(8,128)(2,1)S(1)}, u32[]{:S(2)}, u32[]{:S(2)}) collective-permute-start(bf16[2,256,128]{2,1,0:T(8,128)(2,1)S(1)} %get-tuple-element.251), channel_id=1, source_target_pairs={{120,0},{0,8},{8,16},{16,24},{24,32},{32,40},{40,48},{48,56},{56,6... | collective-permute-start | bytes 393224 | tf_op jit(solution)/shard_map/while/body/eval_jaxpr/ppermute | solution.py:12
  67.5 9.6 %collective-permute-start = (bf16[2,256,128]{2,1,0:T(8,128)(2,1)S(1)}, bf16[2,256,128]{2,1,0:T(8,128)(2,1)S(1)}, u32[]{:S(2)}, u32[]{:S(2)}) collective-permute-start(bf16[2,256,128]{2,1,0:T(8,128)(2,1)S(1)} %get-tuple-element.251), channel_id=1, source_target_pairs={{120,0},{0,8},{8,16},{16,24},{24,32},{32,40},{40,48},{48,56},{56,6... | collective-permute-start | bytes 393224 | tf_op jit(solution)/shard_map/while/body/eval_jaxpr/ppermute | solution.py:12
  79.7 8.7 %collective-permute-start = (bf16[2,256,128]{2,1,0:T(8,128)(2,1)S(1)}, bf16[2,256,128]{2,1,0:T(8,128)(2,1)S(1)}, u32[]{:S(2)}, u32[]{:S(2)}) collective-permute-start(bf16[2,256,128]{2,1,0:T(8,128)(2,1)S(1)} %get-tuple-element.251), channel_id=1, source_target_pairs={{120,0},{0,8},{8,16},{16,24},{24,32},{32,40},{40,48},{48,56},{56,6... | collective-permute-start | bytes 393224 | tf_op jit(solution)/shard_map/while/body/eval_jaxpr/ppermute | solution.py:12
  90.9 8.4 %collective-permute-start = (bf16[2,256,128]{2,1,0:T(8,128)(2,1)S(1)}, bf16[2,256,128]{2,1,0:T(8,128)(2,1)S(1)}, u32[]{:S(2)}, u32[]{:S(2)}) collective-permute-start(bf16[2,256,128]{2,1,0:T(8,128)(2,1)S(1)} %get-tuple-element.251), channel_id=1, source_target_pairs={{120,0},{0,8},{8,16},{16,24},{24,32},{32,40},{40,48},{48,56},{56,6... | collective-permute-start | bytes 393224 | tf_op jit(solution)/shard_map/while/body/eval_jaxpr/ppermute | solution.py:12
  101.8 8.4 %collective-permute-start = (bf16[2,256,128]{2,1,0:T(8,128)(2,1)S(1)}, bf16[2,256,128]{2,1,0:T(8,128)(2,1)S(1)}, u32[]{:S(2)}, u32[]{:S(2)}) collective-permute-start(bf16[2,256,128]{2,1,0:T(8,128)(2,1)S(1)} %get-tuple-element.251), channel_id=1, source_target_pairs={{120,0},{0,8},{8,16},{16,24},{24,32},{32,40},{40,48},{48,56},{56,6... | collective-permute-start | bytes 393224 | tf_op jit(solution)/shard_map/while/body/eval_jaxpr/ppermute | solution.py:12
  112.7 8.4 %collective-permute-start = (bf16[2,256,128]{2,1,0:T(8,128)(2,1)S(1)}, bf16[2,256,128]{2,1,0:T(8,128)(2,1)S(1)}, u32[]{:S(2)}, u32[]{:S(2)}) collective-permute-start(bf16[2,256,128]{2,1,0:T(8,128)(2,1)S(1)} %get-tuple-element.251), channel_id=1, source_target_pairs={{120,0},{0,8},{8,16},{16,24},{24,32},{32,40},{40,48},{48,56},{56,6... | collective-permute-start | bytes 393224 | tf_op jit(solution)/shard_map/while/body/eval_jaxpr/ppermute | solution.py:12
  123.7 8.4 %collective-permute-start = (bf16[2,256,128]{2,1,0:T(8,128)(2,1)S(1)}, bf16[2,256,128]{2,1,0:T(8,128)(2,1)S(1)}, u32[]{:S(2)}, u32[]{:S(2)}) collective-permute-start(bf16[2,256,128]{2,1,0:T(8,128)(2,1)S(1)} %get-tuple-element.251), channel_id=1, source_target_pairs={{120,0},{0,8},{8,16},{16,24},{24,32},{32,40},{40,48},{48,56},{56,6... | collective-permute-start | bytes 393224 | tf_op jit(solution)/shard_map/while/body/eval_jaxpr/ppermute | solution.py:12
  134.5 8.4 %collective-permute-start = (bf16[2,256,128]{2,1,0:T(8,128)(2,1)S(1)}, bf16[2,256,128]{2,1,0:T(8,128)(2,1)S(1)}, u32[]{:S(2)}, u32[]{:S(2)}) collective-permute-start(bf16[2,256,128]{2,1,0:T(8,128)(2,1)S(1)} %get-tuple-element.251), channel_id=1, source_target_pairs={{120,0},{0,8},{8,16},{16,24},{24,32},{32,40},{40,48},{48,56},{56,6... | collective-permute-start | bytes 393224 | tf_op jit(solution)/shard_map/while/body/eval_jaxpr/ppermute | solution.py:12
  145.5 8.4 %collective-permute-start = (bf16[2,256,128]{2,1,0:T(8,128)(2,1)S(1)}, bf16[2,256,128]{2,1,0:T(8,128)(2,1)S(1)}, u32[]{:S(2)}, u32[]{:S(2)}) collective-permute-start(bf16[2,256,128]{2,1,0:T(8,128)(2,1)S(1)} %get-tuple-element.251), channel_id=1, source_target_pairs={{120,0},{0,8},{8,16},{16,24},{24,32},{32,40},{40,48},{48,56},{56,6... | collective-permute-start | bytes 393224 | tf_op jit(solution)/shard_map/while/body/eval_jaxpr/ppermute | solution.py:12
  156.4 8.8 %collective-permute-start = (bf16[2,256,128]{2,1,0:T(8,128)(2,1)S(1)}, bf16[2,256,128]{2,1,0:T(8,128)(2,1)S(1)}, u32[]{:S(2)}, u32[]{:S(2)}) collective-permute-start(bf16[2,256,128]{2,1,0:T(8,128)(2,1)S(1)} %get-tuple-element.251), channel_id=1, source_target_pairs={{120,0},{0,8},{8,16},{16,24},{24,32},{32,40},{40,48},{48,56},{56,6... | collective-permute-start | bytes 393224 | tf_op jit(solution)/shard_map/while/body/eval_jaxpr/ppermute | solution.py:12
  167.7 9.6 %collective-permute-start = (bf16[2,256,128]{2,1,0:T(8,128)(2,1)S(1)}, bf16[2,256,128]{2,1,0:T(8,128)(2,1)S(1)}, u32[]{:S(2)}, u32[]{:S(2)}) collective-permute-start(bf16[2,256,128]{2,1,0:T(8,128)(2,1)S(1)} %get-tuple-element.251), channel_id=1, source_target_pairs={{120,0},{0,8},{8,16},{16,24},{24,32},{32,40},{40,48},{48,56},{56,6... | collective-permute-start | bytes 393224 | tf_op jit(solution)/shard_map/while/body/eval_jaxpr/ppermute | solution.py:12
  179.9 8.4 %collective-permute-start = (bf16[2,256,128]{2,1,0:T(8,128)(2,1)S(1)}, bf16[2,256,128]{2,1,0:T(8,128)(2,1)S(1)}, u32[]{:S(2)}, u32[]{:S(2)}) collective-permute-start(bf16[2,256,128]{2,1,0:T(8,128)(2,1)S(1)} %get-tuple-element.251), channel_id=1, source_target_pairs={{120,0},{0,8},{8,16},{16,24},{24,32},{32,40},{40,48},{48,56},{56,6... | collective-permute-start | bytes 393224 | tf_op jit(solution)/shard_map/while/body/eval_jaxpr/ppermute | solution.py:12
  190.8 8.4 %collective-permute-start = (bf16[2,256,128]{2,1,0:T(8,128)(2,1)S(1)}, bf16[2,256,128]{2,1,0:T(8,128)(2,1)S(1)}, u32[]{:S(2)}, u32[]{:S(2)}) collective-permute-start(bf16[2,256,128]{2,1,0:T(8,128)(2,1)S(1)} %get-tuple-element.251), channel_id=1, source_target_pairs={{120,0},{0,8},{8,16},{16,24},{24,32},{32,40},{40,48},{48,56},{56,6... | collective-permute-start | bytes 393224 | tf_op jit(solution)/shard_map/while/body/eval_jaxpr/ppermute | solution.py:12
Sparse Core Ops, SparseCore 0:
  219.2 35.5 reduce-scatter.1
where the time goes:
time: 262 us
  waiting for transfers between devices  140 us (53%)
  matrix products  31.2 us (12%)
  blocking collectives  23.8 us (9%)
  local copies, waits for them, and re-layouts  23.2 us (9%)
  other arithmetic  16.1 us (6%)
  between operations  13.5 us (5%)
  loops' own time  11 us (4%)
    ppermute x15, waiting for transfers between devices, shifted(): return lax.ppermute(block, axis, route)  105 us
    reduce_scatter x1, waiting for transfers between devices, on_device(): lax.psum_scatter(jnp.dot(merged, out_weight, preferred_element_type=jnp.f...  35.7 us
    all_gather x1, blocking collectives, on_device(): everywhere = lax.all_gather(positions, 'ctx', axis=0, tiled=True)  23.8 us
    dynamic_update_slice x15, local copies, waits for them, and re-layouts, on_device(): _, later = lax.scan(advance_keys, jnp.stack([keys, values]), offsets)  12.7 us
    dot_general x1, matrix products, on_device(): jnp.dot(merged, out_weight, preferred_element_type=jnp.float32)  12 us
    another operation x1, loops' own time, on_device(): _, later = lax.scan(advance_keys, jnp.stack([keys, values]), offsets)  11 us
    dot_general x16, matrix products, attend(): jnp.einsum('grqk,kgd->qgrd', weights.astype(jnp.bfloat16), value_heads, p...  10.4 us
    dynamic_slice x15, local copies, waits for them, and re-layouts, on_device(): _, later = lax.scan(advance_keys, jnp.stack([keys, values]), offsets)  8.83 us
  transfers between devices with their start and end apart: 16, of which 16 were waited for; matrix products, arithmetic and copies ran while one was open for 4% of the time, Pallas kernels for 0%

commit v1 on v0

--- a/solution.py
+++ b/solution.py
@@ -75,7 +75,10 @@
     cycle_size = lax.axis_size("ctx")
     device = lax.axis_index("ctx")
     tok_rows = queries.shape[0]
-    everywhere = lax.all_gather(positions, "ctx", axis=0, tiled=True)
+    devices_2 = lax.axis_size("ctx")
+    blocks = jnp.stack([positions for _ in range(devices_2)])
+    blocks = lax.all_to_all(blocks, "ctx", split_axis=0, concat_axis=0)
+    everywhere = jnp.concatenate(blocks, axis=0)
 
     def block_positions(owner_index):
         return lax.dynamic_slice_in_dim(everywhere, owner_index * tok_rows, tok_rows, 0)

time: 262 us -> 248 us (0.947)
  blocking collectives: 23.8 us -> 0 us
  starting transfers between devices: 2.24 us -> 8.8 us
  waiting for transfers between devices: 140 us -> 143 us
    all_gather x1 -> x0, blocking collectives: 23.8 us -> none  [on_device(): everywhere = lax.all_gather(positions, 'ctx', axis=0, tiled=True)]
    all_to_all x0 -> x1, starting transfers between devices: none -> 7.15 us  [on_device(): blocks = lax.all_to_all(blocks, 'ctx', split_axis=0, concat_axis=0)]
    all_to_all x0 -> x1, waiting for transfers between devices: none -> 3.63 us  [on_device(): blocks = lax.all_to_all(blocks, 'ctx', split_axis=0, concat_axis=0)]
  transfers between devices with their start and end apart: 16 -> 17, of which waited for: 16 -> 17; matrix products, arithmetic and copies ran while one was open for 4% -> 6% of each run, Pallas kernels for 0% -> 0%
where the time goes in v1:
time: 248 us
  waiting for transfers between devices  143 us (58%)
  matrix products  31.2 us (13%)
  local copies, waits for them, and re-layouts  24.3 us (10%)
  other arithmetic  16.1 us (6%)
  between operations  13.6 us (5%)
  loops' own time  11 us (4%)
  starting transfers between devices  8.8 us (4%)
    ppermute x15, waiting for transfers between devices, shifted(): return lax.ppermute(block, axis, route)  103 us
    reduce_scatter x1, waiting for transfers between devices, on_device(): lax.psum_scatter(jnp.dot(merged, out_weight, preferred_element_type=jnp.f...  35.6 us
    dynamic_update_slice x15, local copies, waits for them, and re-layouts, on_device(): _, later = lax.scan(advance_keys, jnp.stack([keys, values]), offsets)  12.7 us
    dot_general x1, matrix products, on_device(): jnp.dot(merged, out_weight, preferred_element_type=jnp.float32)  12 us
    another operation x1, loops' own time, on_device(): _, later = lax.scan(advance_keys, jnp.stack([keys, values]), offsets)  11 us
    dot_general x16, matrix products, attend(): jnp.einsum('grqk,kgd->qgrd', weights.astype(jnp.bfloat16), value_heads, p...  10.4 us
    dynamic_slice x15, local copies, waits for them, and re-layouts, on_device(): _, later = lax.scan(advance_keys, jnp.stack([keys, values]), offsets)  8.83 us
    dot_general x16, matrix products, attend(): jnp.einsum('qgrd,kgd->grqk', query_heads, key_heads, preferred_element_ty...  8.72 us
  transfers between devices with their start and end apart: 17, of which 17 were waited for; matrix products, arithmetic and copies ran while one was open for 6% of the time, Pallas kernels for 0%

profile of v1, /device:TPU:0, one launch (start us, length us, event | category | flops | bytes accessed | tf_op | source)
XLA Modules:
  0.0 247.7 jit_solution(13682648855842971457)
XLA Ops:
  6.5 1.3 stack.11
  7.8 7.1 %all-to-all-start = ((s32[16,1,256]{2,1,0:T(1,128)}), s32[16,1,256]{2,1,0:T(1,128)S(1)}, u32[]{:S(2)}, u32[]{:S(2)}) async-start(s32[16,1,256]{2,1,0:T(1,128)} %stack.11), calls=%async_computation | async-start | bytes 32768 | tf_op jit(solution)/shard_map/all_to_all | solution.py:80
  15.0 0.9 broadcast_compare_fusion.1
  15.9 1.6 fusion.23
  18.1 0.6 fusion.31
  18.9 3.6 %all-to-all-done = s32[16,1,256]{2,1,0:T(1,128)S(1)} async-done(((s32[16,1,256]{2,1,0:T(1,128)}), s32[16,1,256]{2,1,0:T(1,128)S(1)}, u32[]{:S(2)}, u32[]{:S(2)}) %all-to-all-start) | async-done | bytes 16416 | tf_op jit(solution)/shard_map/all_to_all | solution.py:80
  22.6 165.3 %while.18 = (s32[]{:T(128)}, bf16[2,256,128]{2,1,0:T(8,128)(2,1)S(1)}, bf16[15,256,1024]{1,2,0:T(8,128)(2,1)}, f32[15,8,256]{2,1,0:T(8,128)S(1)}, f32[15,8,256]{...) while((s32[]{:T(128)}, ...), condition=%wide.region_5.6_spmd, body=%wide.region_2.5_spmd.sunk | while | flops 275838976 | bytes 9654660 | solution.py:97
  24.6 6.3 %collective-permute-done = bf16[2,256,128]{2,1,0:T(8,128)(2,1)S(1)} collective-permute-done((bf16[2,256,128]{2,1,0:T(8,128)(2,1)S(1)}, bf16[2,256,128]{2,1,0:T(8,128)(2,1)S(1)}, u32[]{:S(2)}, u32[]{:S(2)}) %collective-permute-start) | collective-permute-done | bytes 131104 | tf_op jit(solution)/shard_map/while/body/eval_jaxpr/ppermute | solution.py:12
  31.9 0.7 fusion.63
  32.6 0.8 bitcast_dynamic-update-slice_fusion.6
  33.5 0.6 dynamic_slice.15
  35.0 6.8 %collective-permute-done = bf16[2,256,128]{2,1,0:T(8,128)(2,1)S(1)} collective-permute-done((bf16[2,256,128]{2,1,0:T(8,128)(2,1)S(1)}, bf16[2,256,128]{2,1,0:T(8,128)(2,1)S(1)}, u32[]{:S(2)}, u32[]{:S(2)}) %collective-permute-start) | collective-permute-done | bytes 131104 | tf_op jit(solution)/shard_map/while/body/eval_jaxpr/ppermute | solution.py:12
  42.8 0.7 fusion.63
  43.5 0.8 bitcast_dynamic-update-slice_fusion.6
  44.4 0.6 dynamic_slice.15
  45.9 6.8 %collective-permute-done = bf16[2,256,128]{2,1,0:T(8,128)(2,1)S(1)} collective-permute-done((bf16[2,256,128]{2,1,0:T(8,128)(2,1)S(1)}, bf16[2,256,128]{2,1,0:T(8,128)(2,1)S(1)}, u32[]{:S(2)}, u32[]{:S(2)}) %collective-permute-start) | collective-permute-done | bytes 131104 | tf_op jit(solution)/shard_map/while/body/eval_jaxpr/ppermute | solution.py:12
  53.7 0.7 fusion.63
  54.4 0.9 bitcast_dynamic-update-slice_fusion.6
  55.3 0.6 dynamic_slice.15
  56.8 6.8 %collective-permute-done = bf16[2,256,128]{2,1,0:T(8,128)(2,1)S(1)} collective-permute-done((bf16[2,256,128]{2,1,0:T(8,128)(2,1)S(1)}, bf16[2,256,128]{2,1,0:T(8,128)(2,1)S(1)}, u32[]{:S(2)}, u32[]{:S(2)}) %collective-permute-start) | collective-permute-done | bytes 131104 | tf_op jit(solution)/shard_map/while/body/eval_jaxpr/ppermute | solution.py:12
  64.6 0.7 fusion.63
  65.3 0.9 bitcast_dynamic-update-slice_fusion.6
  66.3 0.6 dynamic_slice.15
  67.7 6.8 %collective-permute-done = bf16[2,256,128]{2,1,0:T(8,128)(2,1)S(1)} collective-permute-done((bf16[2,256,128]{2,1,0:T(8,128)(2,1)S(1)}, bf16[2,256,128]{2,1,0:T(8,128)(2,1)S(1)}, u32[]{:S(2)}, u32[]{:S(2)}) %collective-permute-start) | collective-permute-done | bytes 131104 | tf_op jit(solution)/shard_map/while/body/eval_jaxpr/ppermute | solution.py:12
  75.5 0.7 fusion.63
  76.2 0.8 bitcast_dynamic-update-slice_fusion.6
  77.2 0.6 dynamic_slice.15
  78.6 6.8 %collective-permute-done = bf16[2,256,128]{2,1,0:T(8,128)(2,1)S(1)} collective-permute-done((bf16[2,256,128]{2,1,0:T(8,128)(2,1)S(1)}, bf16[2,256,128]{2,1,0:T(8,128)(2,1)S(1)}, u32[]{:S(2)}, u32[]{:S(2)}) %collective-permute-start) | collective-permute-done | bytes 131104 | tf_op jit(solution)/shard_map/while/body/eval_jaxpr/ppermute | solution.py:12
  86.5 0.7 fusion.63
  87.1 0.9 bitcast_dynamic-update-slice_fusion.6
  88.1 0.6 dynamic_slice.15
  89.5 7.9 %collective-permute-done = bf16[2,256,128]{2,1,0:T(8,128)(2,1)S(1)} collective-permute-done((bf16[2,256,128]{2,1,0:T(8,128)(2,1)S(1)}, bf16[2,256,128]{2,1,0:T(8,128)(2,1)S(1)}, u32[]{:S(2)}, u32[]{:S(2)}) %collective-permute-start) | collective-permute-done | bytes 131104 | tf_op jit(solution)/shard_map/while/body/eval_jaxpr/ppermute | solution.py:12
  98.5 0.7 fusion.63
  99.2 0.8 bitcast_dynamic-update-slice_fusion.6
  100.1 0.6 dynamic_slice.15
  101.5 7.4 %collective-permute-done = bf16[2,256,128]{2,1,0:T(8,128)(2,1)S(1)} collective-permute-done((bf16[2,256,128]{2,1,0:T(8,128)(2,1)S(1)}, bf16[2,256,128]{2,1,0:T(8,128)(2,1)S(1)}, u32[]{:S(2)}, u32[]{:S(2)}) %collective-permute-start) | collective-permute-done | bytes 131104 | tf_op jit(solution)/shard_map/while/body/eval_jaxpr/ppermute | solution.py:12
  110.0 0.7 fusion.63
  110.6 0.9 bitcast_dynamic-update-slice_fusion.6
  113.0 6.8 %collective-permute-done = bf16[2,256,128]{2,1,0:T(8,128)(2,1)S(1)} collective-permute-done((bf16[2,256,128]{2,1,0:T(8,128)(2,1)S(1)}, bf16[2,256,128]{2,1,0:T(8,128)(2,1)S(1)}, u32[]{:S(2)}, u32[]{:S(2)}) %collective-permute-start) | collective-permute-done | bytes 131104 | tf_op jit(solution)/shard_map/while/body/eval_jaxpr/ppermute | solution.py:12
  120.9 0.7 fusion.63
  121.5 0.8 bitcast_dynamic-update-slice_fusion.6
  123.9 6.8 %collective-permute-done = bf16[2,256,128]{2,1,0:T(8,128)(2,1)S(1)} collective-permute-done((bf16[2,256,128]{2,1,0:T(8,128)(2,1)S(1)}, bf16[2,256,128]{2,1,0:T(8,128)(2,1)S(1)}, u32[]{:S(2)}, u32[]{:S(2)}) %collective-permute-start) | collective-permute-done | bytes 131104 | tf_op jit(solution)/shard_map/while/body/eval_jaxpr/ppermute | solution.py:12
  131.8 0.7 fusion.63
  132.4 0.9 bitcast_dynamic-update-slice_fusion.6
  133.4 0.6 dynamic_slice.15
  134.9 6.8 %collective-permute-done = bf16[2,256,128]{2,1,0:T(8,128)(2,1)S(1)} collective-permute-done((bf16[2,256,128]{2,1,0:T(8,128)(2,1)S(1)}, bf16[2,256,128]{2,1,0:T(8,128)(2,1)S(1)}, u32[]{:S(2)}, u32[]{:S(2)}) %collective-permute-start) | collective-permute-done | bytes 131104 | tf_op jit(solution)/shard_map/while/body/eval_jaxpr/ppermute | solution.py:12
  142.7 0.7 fusion.63
  143.4 0.8 bitcast_dynamic-update-slice_fusion.6
  145.8 6.8 %collective-permute-done = bf16[2,256,128]{2,1,0:T(8,128)(2,1)S(1)} collective-permute-done((bf16[2,256,128]{2,1,0:T(8,128)(2,1)S(1)}, bf16[2,256,128]{2,1,0:T(8,128)(2,1)S(1)}, u32[]{:S(2)}, u32[]{:S(2)}) %collective-permute-start) | collective-permute-done | bytes 131104 | tf_op jit(solution)/shard_map/while/body/eval_jaxpr/ppermute | solution.py:12
  153.6 0.7 fusion.63
  154.3 0.8 bitcast_dynamic-update-slice_fusion.6
  156.7 6.8 %collective-permute-done = bf16[2,256,128]{2,1,0:T(8,128)(2,1)S(1)} collective-permute-done((bf16[2,256,128]{2,1,0:T(8,128)(2,1)S(1)}, bf16[2,256,128]{2,1,0:T(8,128)(2,1)S(1)}, u32[]{:S(2)}, u32[]{:S(2)}) %collective-permute-start) | collective-permute-done | bytes 131104 | tf_op jit(solution)/shard_map/while/body/eval_jaxpr/ppermute | solution.py:12
  164.5 0.7 fusion.63
  165.2 0.8 bitcast_dynamic-update-slice_fusion.6
  166.1 0.6 dynamic_slice.15
  167.6 6.8 %collective-permute-done = bf16[2,256,128]{2,1,0:T(8,128)(2,1)S(1)} collective-permute-done((bf16[2,256,128]{2,1,0:T(8,128)(2,1)S(1)}, bf16[2,256,128]{2,1,0:T(8,128)(2,1)S(1)}, u32[]{:S(2)}, u32[]{:S(2)}) %collective-permute-start) | collective-permute-done | bytes 131104 | tf_op jit(solution)/shard_map/while/body/eval_jaxpr/ppermute | solution.py:12
  175.4 0.7 fusion.63
  176.1 0.9 bitcast_dynamic-update-slice_fusion.6
  178.5 6.8 %collective-permute-done = bf16[2,256,128]{2,1,0:T(8,128)(2,1)S(1)} collective-permute-done((bf16[2,256,128]{2,1,0:T(8,128)(2,1)S(1)}, bf16[2,256,128]{2,1,0:T(8,128)(2,1)S(1)}, u32[]{:S(2)}, u32[]{:S(2)}) %collective-permute-start) | collective-permute-done | bytes 131104 | tf_op jit(solution)/shard_map/while/body/eval_jaxpr/ppermute | solution.py:12
  186.4 0.7 fusion.63
  187.0 0.8 bitcast_dynamic-update-slice_fusion.6
  188.0 5.2 %multiply_reduce_fusion = bf16[256,8,128]{0,2,1:T(8,128)(2,1)S(1)} fusion(bf16[15,256,8,128]{1,3,2,0:T(8,128)(2,1)} %bitcast.169, bf16[1,256,8,128]{1,3,2,0:T(8,128)(2,1)S(1)} %bitcast.171, f32[16,256,8]{1,2,0:T(8,128)S(1)} %divide_bitcast_fusion), kind=kLoop, calls=%fused_computation.28 | loop fusion | flops 24903680 | bytes 9043968 | tf_op jit(solution)/shard_map/reduce_sum | solution.py:57
  193.2 12.0 %convolution_convert_fusion = bf16[256,8192]{1,0:T(8,128)(2,1)} fusion(bf16[256,1024]{0,1:T(8,128)(2,1)S(1)} %bitcast.170, bf16[1024,8192]{1,0:T(8,128)(2,1)} %param.11), kind=kOutput, calls=%fused_computation.29 | convolution fusion | flops 4297064448 | bytes 21495808 | tf_op jit(solution)/shard_map/dot_general | solution.py:101
  205.2 35.6 %reduce-scatter.2.cloned.1.call-done = bf16[32,8192]{1,0:T(8,128)(2,1)} async-done(((bf16[256,8192]{1,0:T(8,128)(2,1)}), bf16[32,8192]{1,0:T(8,128)(2,1)}) %reduce-scatter.2.cloned.1.call-update) | async-done | bytes 524304 | tf_op jit(solution)/shard_map/reduce_scatter | solution.py:100
  (132 shorter events, 23.9 us)
Async XLA Ops:
  7.8 14.8 %all-to-all-start = ((s32[16,1,256]{2,1,0:T(1,128)}), s32[16,1,256]{2,1,0:T(1,128)S(1)}, u32[]{:S(2)}, u32[]{:S(2)}) async-start(s32[16,1,256]{2,1,0:T(1,128)} %stack.11), calls=%async_computation | async-start | bytes 32768 | tf_op jit(solution)/shard_map/all_to_all | solution.py:80
  15.0 225.9 %reduce-scatter.2.cloned.1.call-start = ((), (), s32[]{:S(2)}) async-start(), calls=%async_computation.2 | async-start | bytes 4718592 | tf_op jit(solution)/shard_map/reduce_scatter | solution.py:100
  15.9 2.1 copy-start.3
  18.0 0.8 copy-start.1
  18.1 4.5 %copy-start = (bf16[256,1024]{1,0:T(8,128)(2,1)S(1)}, bf16[256,1024]{1,0:T(8,128)(2,1)}, u32[]{:S(2)}) copy-start(bf16[256,1024]{1,0:T(8,128)(2,1)} %param.7) | copy-start | bytes 1572868
  18.1 4.5 %copy-start.2 = (s32[256]{0:T(256)S(1)}, s32[256]{0:T(256)}, u32[]{:S(2)}) copy-start(s32[256]{0:T(256)} %param.10) | copy-start | bytes 3076
  22.6 8.3 %collective-permute-start = (bf16[2,256,128]{2,1,0:T(8,128)(2,1)S(1)}, bf16[2,256,128]{2,1,0:T(8,128)(2,1)S(1)}, u32[]{:S(2)}, u32[]{:S(2)}) collective-permute-start(bf16[2,256,128]{2,1,0:T(8,128)(2,1)S(1)} %get-tuple-element.251), channel_id=1, source_target_pairs={{120,0},{0,8},{8,16},{16,24},{24,32},{32,40},{40,48},{48,56},{56,6... | collective-permute-start | bytes 393224 | tf_op jit(solution)/shard_map/while/body/eval_jaxpr/ppermute | solution.py:12
  33.4 8.4 %collective-permute-start = (bf16[2,256,128]{2,1,0:T(8,128)(2,1)S(1)}, bf16[2,256,128]{2,1,0:T(8,128)(2,1)S(1)}, u32[]{:S(2)}, u32[]{:S(2)}) collective-permute-start(bf16[2,256,128]{2,1,0:T(8,128)(2,1)S(1)} %get-tuple-element.251), channel_id=1, source_target_pairs={{120,0},{0,8},{8,16},{16,24},{24,32},{32,40},{40,48},{48,56},{56,6... | collective-permute-start | bytes 393224 | tf_op jit(solution)/shard_map/while/body/eval_jaxpr/ppermute | solution.py:12
  44.3 8.4 %collective-permute-start = (bf16[2,256,128]{2,1,0:T(8,128)(2,1)S(1)}, bf16[2,256,128]{2,1,0:T(8,128)(2,1)S(1)}, u32[]{:S(2)}, u32[]{:S(2)}) collective-permute-start(bf16[2,256,128]{2,1,0:T(8,128)(2,1)S(1)} %get-tuple-element.251), channel_id=1, source_target_pairs={{120,0},{0,8},{8,16},{16,24},{24,32},{32,40},{40,48},{48,56},{56,6... | collective-permute-start | bytes 393224 | tf_op jit(solution)/shard_map/while/body/eval_jaxpr/ppermute | solution.py:12
  55.3 8.4 %collective-permute-start = (bf16[2,256,128]{2,1,0:T(8,128)(2,1)S(1)}, bf16[2,256,128]{2,1,0:T(8,128)(2,1)S(1)}, u32[]{:S(2)}, u32[]{:S(2)}) collective-permute-start(bf16[2,256,128]{2,1,0:T(8,128)(2,1)S(1)} %get-tuple-element.251), channel_id=1, source_target_pairs={{120,0},{0,8},{8,16},{16,24},{24,32},{32,40},{40,48},{48,56},{56,6... | collective-permute-start | bytes 393224 | tf_op jit(solution)/shard_map/while/body/eval_jaxpr/ppermute | solution.py:12
  66.2 8.4 %collective-permute-start = (bf16[2,256,128]{2,1,0:T(8,128)(2,1)S(1)}, bf16[2,256,128]{2,1,0:T(8,128)(2,1)S(1)}, u32[]{:S(2)}, u32[]{:S(2)}) collective-permute-start(bf16[2,256,128]{2,1,0:T(8,128)(2,1)S(1)} %get-tuple-element.251), channel_id=1, source_target_pairs={{120,0},{0,8},{8,16},{16,24},{24,32},{32,40},{40,48},{48,56},{56,6... | collective-permute-start | bytes 393224 | tf_op jit(solution)/shard_map/while/body/eval_jaxpr/ppermute | solution.py:12
  77.1 8.4 %collective-permute-start = (bf16[2,256,128]{2,1,0:T(8,128)(2,1)S(1)}, bf16[2,256,128]{2,1,0:T(8,128)(2,1)S(1)}, u32[]{:S(2)}, u32[]{:S(2)}) collective-permute-start(bf16[2,256,128]{2,1,0:T(8,128)(2,1)S(1)} %get-tuple-element.251), channel_id=1, source_target_pairs={{120,0},{0,8},{8,16},{16,24},{24,32},{32,40},{40,48},{48,56},{56,6... | collective-permute-start | bytes 393224 | tf_op jit(solution)/shard_map/while/body/eval_jaxpr/ppermute | solution.py:12
  88.0 9.5 %collective-permute-start = (bf16[2,256,128]{2,1,0:T(8,128)(2,1)S(1)}, bf16[2,256,128]{2,1,0:T(8,128)(2,1)S(1)}, u32[]{:S(2)}, u32[]{:S(2)}) collective-permute-start(bf16[2,256,128]{2,1,0:T(8,128)(2,1)S(1)} %get-tuple-element.251), channel_id=1, source_target_pairs={{120,0},{0,8},{8,16},{16,24},{24,32},{32,40},{40,48},{48,56},{56,6... | collective-permute-start | bytes 393224 | tf_op jit(solution)/shard_map/while/body/eval_jaxpr/ppermute | solution.py:12
  100.0 8.9 %collective-permute-start = (bf16[2,256,128]{2,1,0:T(8,128)(2,1)S(1)}, bf16[2,256,128]{2,1,0:T(8,128)(2,1)S(1)}, u32[]{:S(2)}, u32[]{:S(2)}) collective-permute-start(bf16[2,256,128]{2,1,0:T(8,128)(2,1)S(1)} %get-tuple-element.251), channel_id=1, source_target_pairs={{120,0},{0,8},{8,16},{16,24},{24,32},{32,40},{40,48},{48,56},{56,6... | collective-permute-start | bytes 393224 | tf_op jit(solution)/shard_map/while/body/eval_jaxpr/ppermute | solution.py:12
  111.5 8.4 %collective-permute-start = (bf16[2,256,128]{2,1,0:T(8,128)(2,1)S(1)}, bf16[2,256,128]{2,1,0:T(8,128)(2,1)S(1)}, u32[]{:S(2)}, u32[]{:S(2)}) collective-permute-start(bf16[2,256,128]{2,1,0:T(8,128)(2,1)S(1)} %get-tuple-element.251), channel_id=1, source_target_pairs={{120,0},{0,8},{8,16},{16,24},{24,32},{32,40},{40,48},{48,56},{56,6... | collective-permute-start | bytes 393224 | tf_op jit(solution)/shard_map/while/body/eval_jaxpr/ppermute | solution.py:12
  122.4 8.4 %collective-permute-start = (bf16[2,256,128]{2,1,0:T(8,128)(2,1)S(1)}, bf16[2,256,128]{2,1,0:T(8,128)(2,1)S(1)}, u32[]{:S(2)}, u32[]{:S(2)}) collective-permute-start(bf16[2,256,128]{2,1,0:T(8,128)(2,1)S(1)} %get-tuple-element.251), channel_id=1, source_target_pairs={{120,0},{0,8},{8,16},{16,24},{24,32},{32,40},{40,48},{48,56},{56,6... | collective-permute-start | bytes 393224 | tf_op jit(solution)/shard_map/while/body/eval_jaxpr/ppermute | solution.py:12
  133.3 8.4 %collective-permute-start = (bf16[2,256,128]{2,1,0:T(8,128)(2,1)S(1)}, bf16[2,256,128]{2,1,0:T(8,128)(2,1)S(1)}, u32[]{:S(2)}, u32[]{:S(2)}) collective-permute-start(bf16[2,256,128]{2,1,0:T(8,128)(2,1)S(1)} %get-tuple-element.251), channel_id=1, source_target_pairs={{120,0},{0,8},{8,16},{16,24},{24,32},{32,40},{40,48},{48,56},{56,6... | collective-permute-start | bytes 393224 | tf_op jit(solution)/shard_map/while/body/eval_jaxpr/ppermute | solution.py:12
  144.2 8.4 %collective-permute-start = (bf16[2,256,128]{2,1,0:T(8,128)(2,1)S(1)}, bf16[2,256,128]{2,1,0:T(8,128)(2,1)S(1)}, u32[]{:S(2)}, u32[]{:S(2)}) collective-permute-start(bf16[2,256,128]{2,1,0:T(8,128)(2,1)S(1)} %get-tuple-element.251), channel_id=1, source_target_pairs={{120,0},{0,8},{8,16},{16,24},{24,32},{32,40},{40,48},{48,56},{56,6... | collective-permute-start | bytes 393224 | tf_op jit(solution)/shard_map/while/body/eval_jaxpr/ppermute | solution.py:12
  155.1 8.4 %collective-permute-start = (bf16[2,256,128]{2,1,0:T(8,128)(2,1)S(1)}, bf16[2,256,128]{2,1,0:T(8,128)(2,1)S(1)}, u32[]{:S(2)}, u32[]{:S(2)}) collective-permute-start(bf16[2,256,128]{2,1,0:T(8,128)(2,1)S(1)} %get-tuple-element.251), channel_id=1, source_target_pairs={{120,0},{0,8},{8,16},{16,24},{24,32},{32,40},{40,48},{48,56},{56,6... | collective-permute-start | bytes 393224 | tf_op jit(solution)/shard_map/while/body/eval_jaxpr/ppermute | solution.py:12
  166.1 8.4 %collective-permute-start = (bf16[2,256,128]{2,1,0:T(8,128)(2,1)S(1)}, bf16[2,256,128]{2,1,0:T(8,128)(2,1)S(1)}, u32[]{:S(2)}, u32[]{:S(2)}) collective-permute-start(bf16[2,256,128]{2,1,0:T(8,128)(2,1)S(1)} %get-tuple-element.251), channel_id=1, source_target_pairs={{120,0},{0,8},{8,16},{16,24},{24,32},{32,40},{40,48},{48,56},{56,6... | collective-permute-start | bytes 393224 | tf_op jit(solution)/shard_map/while/body/eval_jaxpr/ppermute | solution.py:12
  177.0 8.4 %collective-permute-start = (bf16[2,256,128]{2,1,0:T(8,128)(2,1)S(1)}, bf16[2,256,128]{2,1,0:T(8,128)(2,1)S(1)}, u32[]{:S(2)}, u32[]{:S(2)}) collective-permute-start(bf16[2,256,128]{2,1,0:T(8,128)(2,1)S(1)} %get-tuple-element.251), channel_id=1, source_target_pairs={{120,0},{0,8},{8,16},{16,24},{24,32},{32,40},{40,48},{48,56},{56,6... | collective-permute-start | bytes 393224 | tf_op jit(solution)/shard_map/while/body/eval_jaxpr/ppermute | solution.py:12
Sparse Core Ops, SparseCore 0:
  205.3 35.4 reduce-scatter.1
